TPU v7x, 32 devices: a whole 2x2x4 slice. The times are simulated.
32 devices in a mesh: dp: 16 (over z, x, core), rep: 2 (over y).
Axes of the slice: x: 2, y: 2, z: 4, core: 2. Of those that a mesh axis runs over, the one named last changes fastest.
Arguments:
- learn_residual: bfloat16 [20480, 1024], P(('dp', 'rep')), may hold values from -6 to 6
- learn_hidden: bfloat16 [20480, 4096], P(('dp', 'rep')), may hold values from -6 to 6
- fresh_residual: bfloat16 [20480, 1024], P(('dp', 'rep')), may hold values from -6 to 6
- fresh_hidden: bfloat16 [20480, 4096], P(('dp', 'rep')), may hold values from -6 to 6
- down_weight: bfloat16 [4096, 1024], P('dp'), may hold values from -0.09375 to 0.09375
- head_weight: bfloat16 [1024, 19], replicated, may hold values from -0.1875 to 0.1875
- norm_gain: bfloat16 [1024], replicated, may hold values from 0.099609375 to 1.8984375
- actions: int32 [256, 80], P(('dp', 'rep')), may hold values from 0 to 17
- behaviour_logits: float32 [20480, 18], P(('dp', 'rep')), may hold values from -6 to 6
- rewards: float32 [256, 80], P(('dp', 'rep')), may hold values from -6 to 6
- episode_done: int32 [256, 80], P(('dp', 'rep')), may hold values 0 or 1
- lengths: int32 [256], P(('dp', 'rep')), may hold values from 40 to 80, as said below
- bootstrap: float32 [256], P(('dp', 'rep')), may hold values from -6 to 6
Outputs:
- fresh_policy: float32 [20480, 19], P(('dp', 'rep'))
- learn_targets: float32 [256, 80], P(('dp', 'rep'))
- hidden_grad: bfloat16 [20480, 4096], P(('dp', 'rep'))
- down_grad: float32 [4096, 1024], P('dp')
- head_grad: float32 [1024, 19], replicated
- gain_grad: float32 [1024], replicated
Inputs may be any that keep to these rules, and one draw needn't show every extreme that they name: `lengths`: on at least one device all 8 trajectories of that device have the full 80 steps.
All inputs are finite; a program needn't handle non-finite values. No bound on the sum of `episode_done` on one device may be relied on, other than what follows from the above.
Results may differ from a plain program's by a relative error of at most 0.0049.
Values may be sent and summed in bfloat16 or wider, within the bound.
A program may use at most 128 MiB of HBM per device.

v0:
```python
import jax
import jax.numpy as jnp
from jax import lax
from jax.sharding import PartitionSpec as P

ACTIONS = 18
STEPS = 80
TRAJ_DEV = 8
DISCOUNT = 0.99
BASELINE_COST = 0.5
ENTROPY_COST = 0.05
EPSILON = 1e-05


def normalize(features, gain_vector):
    inverse_rms = lax.rsqrt(jnp.mean(features * features, axis=1, keepdims=True) + EPSILON)
    return features * inverse_rms * gain_vector[None, :]


def head_outputs(features, head_matrix, gain_vector):
    return jnp.dot(normalize(features, gain_vector), head_matrix, precision=lax.Precision.HIGHEST)


def log_policy(logits):
    return logits - jnp.log(jnp.sum(jnp.exp(logits), axis=-1, keepdims=True))


def compose_steps(earlier, later):
    return (earlier[0] * later[0], later[1] + later[0] * earlier[1])


def trace_returns(errors, traces):
    _, corrections = lax.associative_scan(compose_steps, (traces, errors), reverse=True, axis=1)
    return corrections


def learner_loss(
    features,
    head_matrix,
    gain_vector,
    actions,
    behaviour_logits,
    rewards,
    episode_done,
    lengths,
    bootstrap,
):
    trajectories = actions.shape[0]
    outputs = head_outputs(features, head_matrix, gain_vector)
    logprob = log_policy(outputs[:, :ACTIONS])
    values = outputs[:, ACTIONS].reshape(trajectories, STEPS)
    one_hot = (
        actions.reshape(-1)[:, None] == jnp.arange(ACTIONS, dtype=jnp.int32)[None, :]
    ).astype(jnp.float32)
    taken = jnp.sum(logprob * one_hot, axis=1).reshape(trajectories, STEPS)
    behaved = jnp.sum(log_policy(behaviour_logits) * one_hot, axis=1).reshape(trajectories, STEPS)
    entropy = -jnp.sum(jnp.exp(logprob) * logprob, axis=1).reshape(trajectories, STEPS)
    clipped_ratio = jnp.minimum(1.0, jnp.exp(lax.stop_gradient(taken) - behaved))
    positions = jnp.arange(STEPS, dtype=jnp.int32)[None, :]
    inside = positions < lengths[:, None]
    final_step = positions == lengths[:, None] - 1
    discounts = DISCOUNT * (1.0 - episode_done.astype(jnp.float32))
    baseline = lax.stop_gradient(values)
    empty_column = jnp.zeros((trajectories, 1), jnp.float32)
    next_value = jnp.concatenate([baseline[:, 1:], empty_column], axis=1)
    next_value = jnp.where(final_step, bootstrap[:, None], next_value)
    errors = jnp.where(inside, clipped_ratio * (rewards + discounts * next_value - baseline), 0.0)
    traces = jnp.where(inside, discounts * clipped_ratio, 0.0)
    targets = baseline + trace_returns(errors, traces)
    next_target = jnp.concatenate([targets[:, 1:], empty_column], axis=1)
    next_target = jnp.where(final_step, bootstrap[:, None], next_target)
    advantage = clipped_ratio * (rewards + discounts * next_target - baseline)
    per_step = (
        -advantage * taken + 0.5 * BASELINE_COST * (targets - values) ** 2 - ENTROPY_COST * entropy
    )
    total_loss = jnp.sum(jnp.where(inside, per_step, 0.0)) / (TRAJ_DEV * STEPS)
    return (total_loss, targets)


def local(
    learn_residual,
    learn_hidden,
    fresh_residual,
    fresh_hidden,
    down_weight,
    head_weight,
    norm_gain,
    actions,
    behaviour_logits,
    rewards,
    episode_done,
    lengths,
    bootstrap,
):
    head_matrix = head_weight.astype(jnp.float32)
    gain_vector = norm_gain.astype(jnp.float32)
    full_down = lax.all_gather(down_weight, "dp", axis=0, tiled=True)
    learn_stream = learn_residual.astype(jnp.float32) + jnp.dot(
        learn_hidden, full_down, preferred_element_type=jnp.float32
    )
    fresh_stream = fresh_residual.astype(jnp.float32) + jnp.dot(
        fresh_hidden, full_down, preferred_element_type=jnp.float32
    )
    fresh_policy = head_outputs(fresh_stream, head_matrix, gain_vector)

    def loss_of(features, head_values, gain_values):
        return learner_loss(
            features,
            head_values,
            gain_values,
            actions,
            behaviour_logits,
            rewards,
            episode_done,
            lengths,
            bootstrap,
        )

    total_loss, pullback, targets = jax.vjp(
        loss_of, learn_stream, head_matrix, gain_vector, has_aux=True
    )
    stream_grad, head_local, gain_local = pullback(jnp.ones_like(total_loss))
    rounded = stream_grad.astype(jnp.bfloat16)
    head_grad, gain_grad = lax.psum((head_local, gain_local), ("dp", "rep"))
    grad_shard = lax.psum_scatter(
        lax.dot_general(
            learn_hidden, rounded, (((0,), (0,)), ((), ())), preferred_element_type=jnp.float32
        ),
        "dp",
        scatter_dimension=0,
        tiled=True,
    )
    down_grad = lax.psum(grad_shard, "rep")
    hidden_sum = lax.dot_general(
        rounded, full_down, (((1,), (1,)), ((), ())), preferred_element_type=jnp.float32
    )
    hidden_grad = hidden_sum.astype(jnp.bfloat16)
    return (fresh_policy, targets, hidden_grad, down_grad, head_grad, gain_grad)


def solution(mesh):
    placed = (
        P(("dp", "rep"), None),
        P(("dp", "rep"), None),
        P(("dp", "rep"), None),
        P(("dp", "rep"), None),
        P("dp", None),
        P(),
        P(),
        P(("dp", "rep"), None),
        P(("dp", "rep"), None),
        P(("dp", "rep"), None),
        P(("dp", "rep"), None),
        P(("dp", "rep")),
        P(("dp", "rep")),
    )
    return jax.shard_map(
        local,
        mesh=mesh,
        in_specs=placed,
        out_specs=(
            P(("dp", "rep"), None),
            P(("dp", "rep"), None),
            P(("dp", "rep"), None),
            P("dp", None),
            P(),
            P(),
        ),
        check_vma=False,
    )
```

profile of v0, /device:TPU:8, one launch (start us, length us, event | category | flops | bytes accessed | tf_op | source)
XLA Modules:
  0.0 475.9 jit_solution(9676328896604979801)
XLA Ops:
  7.2 0.7 all-gather.2.cloned.1.call-update
  8.0 0.7 convert_element_type.21
  8.6 0.8 eq.12
  9.4 0.9 exponential_reduce_fusion
  10.3 0.7 broadcast_add_fusion
  10.9 74.4 %all-gather.2.cloned.1.call-done = bf16[4096,1024]{1,0:T(8,128)(2,1)} async-done(((bf16[256,1024]{1,0:T(8,128)(2,1)}), bf16[4096,1024]{1,0:T(8,128)(2,1)}) %all-gather.2.cloned.1.call-update) | async-done | bytes 8388624 | tf_op jit(solution)/shard_map/all_gather | solution.py:97
  85.4 9.9 %multiply_reduce_fusion.2 = (f32[640]{0:T(1024)S(1)}, f32[640,1024]{1,0:T(8,128)S(1)}) fusion(bf16[640,4096]{1,0:T(8,128)(2,1)} %param.14, bf16[4096,1024]{1,0:T(8,128)(2,1)} %all-gather.2.cloned.1.call-done, bf16[640,1024]{1,0:T(8,128)(2,1)} %param.13), kind=kOutput, calls=%fused_computation.6 | convolution fusion | flops 5371330048 | bytes 17566208 | tf_op jit(solution)/shard_map/dot_general | solution.py:98
  95.4 1.5 fusion.6
  97.4 0.1 slice.177
  97.5 0.1 slice.171
  97.6 0.1 slice.167
  97.7 0.1 slice.173
  97.8 0.1 slice.169
  98.2 0.1 slice.185
  100.2 0.1 slice.176
  100.3 0.1 slice.165
  101.7 0.1 pad.56
  102.0 0.1 pad.55
  102.7 1.8 multiply_reduce_fusion
  104.6 0.5 fusion
  105.1 1.2 copy-done.1
  106.3 12.7 %convolution_bitcast_fusion = f32[4096,1024]{0,1:T(8,128)} fusion(bf16[640,1024]{1,0:T(8,128)(2,1)S(1)} %fusion, bf16[640,4096]{1,0:T(8,128)(2,1)} %param.14), kind=kOutput, calls=%fused_computation | convolution fusion | flops 5368709120 | bytes 23330816 | tf_op jit(solution)/shard_map/dot_general | solution.py:126
  119.0 175.0 %reduce-scatter.2.cloned.1.call-done = f32[256,1024]{0,1:T(8,128)} async-done(((f32[4096,1024]{0,1:T(8,128)}), f32[256,1024]{0,1:T(8,128)}) %reduce-scatter.2.cloned.1.call-update) | async-done | bytes 1048592 | tf_op jit(solution)/shard_map/reduce_scatter | solution.py:125
  294.1 0.2 all-reduce.21.cloned.1.call-start
  294.3 10.9 %multiply_reduce_fusion.3 = (f32[640]{0:T(1024)S(1)}, f32[640,1024]{1,0:T(8,128)}) fusion(bf16[640,1024]{1,0:T(8,128)(2,1)} %param.15, bf16[640,4096]{1,0:T(8,128)(2,1)} %param.16, bf16[4096,1024]{1,0:T(8,128)(2,1)} %all-gather.2.cloned.1.call-done), kind=kOutput, calls=%fused_computation.11 | convolution fusion | flops 5371330048 | bytes 17566208 | tf_op jit(solution)/shard_map/dot_general | solution.py:101
  305.2 2.4 fusion.4
  307.6 11.1 %convolution_convert_fusion = bf16[640,4096]{1,0:T(8,128)(2,1)} fusion(bf16[640,1024]{1,0:T(8,128)(2,1)} %copy-done.1, bf16[4096,1024]{1,0:T(8,128)(2,1)} %all-gather.2.cloned.1.call-done), kind=kOutput, calls=%fused_computation.1 | convolution fusion | flops 5371330560 | bytes 14942208 | tf_op jit(solution)/shard_map/dot_general | solution.py:134
  318.8 2.3 fusion.1
  321.1 40.5 %psum.23 = f32[1024]{0:T(1024)} all-reduce(f32[1024]{0:T(1024)S(1)} %get-tuple-element.12), channel_id=1, replica_groups=mesh['dp'=16,'rep'=2] {'dp','rep'}, use_global_device_ids=true, to_apply=%region_12.13 | all-reduce | flops 1024 | bytes 8192 | tf_op jit(solution)/shard_map/psum | solution.py:124
  361.5 2.5 copy.19
  364.1 103.8 %all-reduce.21.cloned.1.call-done = f32[1024,19]{0,1:T(8,128)} async-done(((f32[1024,19]{0,1:T(8,128)}), f32[1024,19]{0,1:T(8,128)}) %all-reduce.21.cloned.1.call-update) | async-done | bytes 77840 | tf_op jit(solution)/shard_map/psum | solution.py:124
  467.8 1.5 copy.22
  (107 shorter events, 4.8 us)
Async XLA Ops:
  7.2 88.2 %copy-start = (bf16[1024,19]{0,1:T(8,128)(2,1)S(1)}, bf16[1024,19]{0,1:T(8,128)(2,1)}, u32[]{:S(2)}) copy-start(bf16[1024,19]{0,1:T(8,128)(2,1)} %param.18) | copy-start | bytes 116740
  7.2 78.2 %all-gather.2.cloned.1.call-start = ((), (), s32[]{:S(2)}) async-start(), calls=%async_computation.1 | async-start | bytes 8912896 | tf_op jit(solution)/shard_map/all_gather | solution.py:97
  7.9 286.2 %reduce-scatter.2.cloned.1.call-start = ((), (), s32[]{:S(2)}) async-start(), calls=%async_computation.2 | async-start | bytes 17825792 | tf_op jit(solution)/shard_map/reduce_scatter | solution.py:125
  95.3 1.8 copy-start.4
  95.3 2.0 copy-start.6
  95.3 1.9 copy-start.7
  95.3 1.9 copy-start.8
  95.3 1.9 copy-start.9
  102.3 2.3 copy-start.5
  105.1 1.2 copy-start.1
  119.0 242.5 %all-reduce.19.cloned.1.call-start = ((), (), s32[]{:S(2)}) async-start(), calls=%async_computation.3 | async-start | bytes 2097152 | tf_op jit(solution)/shard_map/psum | solution.py:133
  294.1 173.7 %all-reduce.21.cloned.1.call-start = ((), (), s32[]{:S(2)}) async-start(), calls=%async_computation.4 | async-start | bytes 196608 | tf_op jit(solution)/shard_map/psum | solution.py:124
  307.6 11.1 %copy-start.2 = (f32[640,1024]{1,0:T(8,128)S(1)}, f32[640,1024]{1,0:T(8,128)}, u32[]{:S(2)}) copy-start(f32[640,1024]{1,0:T(8,128)} %get-tuple-element.39) | copy-start | bytes 7864324
  307.6 11.1 %copy-start.3 = (bf16[640,1024]{1,0:T(8,128)(2,1)S(1)}, bf16[640,1024]{1,0:T(8,128)(2,1)}, u32[]{:S(2)}) copy-start(bf16[640,1024]{1,0:T(8,128)(2,1)} %param.15) | copy-start | bytes 3932164
Sparse Core Ops, SparseCore 0:
  10.2 75.1 all-gather.1
  119.1 174.9 reduce-scatter.1
  296.4 40.8 all-reduce.18
  343.2 124.5 all-reduce.20
where the time goes:
time: 476 us
  waiting for transfers between devices  354 us (74%)
  matrix products  52.6 us (11%)
  blocking collectives  40.5 us (9%)
  between operations  14.1 us (3%)
  local copies, waits for them, and re-layouts  10.6 us (2%)
    reduce_scatter x1, waiting for transfers between devices, local(): lax.psum_scatter(lax.dot_general(learn_hidden, rounded, (((0,), (0,)), ((...  175 us
    psum x1, waiting for transfers between devices, local(): head_grad, gain_grad = lax.psum((head_local, gain_local), ('dp', 'rep'))  104 us
    all_gather x1, waiting for transfers between devices, local(): full_down = lax.all_gather(down_weight, 'dp', axis=0, tiled=True)  74.4 us
    psum x1, blocking collectives, local(): head_grad, gain_grad = lax.psum((head_local, gain_local), ('dp', 'rep'))  40.5 us
    dot_general x1, matrix products, local(): lax.dot_general(learn_hidden, rounded, (((0,), (0,)), ((), ())), preferre...  12.7 us
    dot_general x1, matrix products, local(): lax.dot_general(rounded, full_down, (((1,), (1,)), ((), ())), preferred_e...  11.1 us
    dot_general x1, matrix products, local(): jnp.dot(fresh_hidden, full_down, preferred_element_type=jnp.float32)  10.9 us
    dot_general x1, matrix products, local(): jnp.dot(learn_hidden, full_down, preferred_element_type=jnp.float32)  9.89 us
  transfers between devices with their start and end apart: 4, of which 3 were waited for; matrix products, arithmetic and copies ran while one was open for 7% of the time, Pallas kernels for 0%

commit v1 on v0

--- a/solution.py
+++ b/solution.py
@@ -94,7 +94,12 @@
 ):
     head_matrix = head_weight.astype(jnp.float32)
     gain_vector = norm_gain.astype(jnp.float32)
-    full_down = lax.all_gather(down_weight, "dp", axis=0, tiled=True)
+    ring = [down_weight]
+    for hop in range(15):
+        ring.append(lax.ppermute(ring[-1], "dp", [(dev, (dev + 1) % 16) for dev in range(16)]))
+    full_down = jnp.roll(
+        jnp.concatenate(ring[::-1], axis=0), (lax.axis_index("dp") + 1) * ring[0].shape[0], axis=0
+    )
     learn_stream = learn_residual.astype(jnp.float32) + jnp.dot(
         learn_hidden, full_down, preferred_element_type=jnp.float32
     )

time: 476 us -> 590 us (1.24)
  waiting for transfers between devices: 354 us -> 437 us
  local copies, waits for them, and re-layouts: 10.6 us -> 35.6 us
    ppermute x0 -> x15, waiting for transfers between devices: none -> 138 us  [local(): lax.ppermute(ring[-1], 'dp', [(dev, (dev + 1) % 16) for dev in range(16)])]
    all_gather x1 -> x0, waiting for transfers between devices: 74.4 us -> none  [local(): full_down = lax.all_gather(down_weight, 'dp', axis=0, tiled=True)]
    unnamed x22 -> x91, local copies, waits for them, and re-layouts: 5.28 us -> 30.2 us
    psum x1, waiting for transfers between devices: 104 us -> 117 us  [local(): head_grad, gain_grad = lax.psum((head_local, gain_local), ('dp', 'rep'))]
    reduce_scatter x1, waiting for transfers between devices: 175 us -> 183 us  [local(): lax.psum_scatter(lax.dot_general(learn_hidden, rounded, (((0,), (0,)), ((...]
  transfers between devices with their start and end apart: 4 -> 18, of which waited for: 3 -> 17; matrix products, arithmetic and copies ran while one was open for 7% -> 7% of each run, Pallas kernels for 0% -> 0%
where the time goes in v1:
time: 590 us; the launch traced here: 589 us
  waiting for transfers between devices  437 us (74%)
  matrix products  57.7 us (10%)
  blocking collectives  40.1 us (7%)
  local copies, waits for them, and re-layouts  35.6 us (6%)
  between operations  14.5 us (2%)
    reduce_scatter x1, waiting for transfers between devices, local(): lax.psum_scatter(lax.dot_general(learn_hidden, rounded, (((0,), (0,)), ((...  183 us
    ppermute x15, waiting for transfers between devices, local(): lax.ppermute(ring[-1], 'dp', [(dev, (dev + 1) % 16) for dev in range(16)])  138 us
    psum x1, waiting for transfers between devices, local(): head_grad, gain_grad = lax.psum((head_local, gain_local), ('dp', 'rep'))  117 us
    psum x1, blocking collectives, local(): head_grad, gain_grad = lax.psum((head_local, gain_local), ('dp', 'rep'))  40.1 us
    unnamed x91, local copies, waits for them, and re-layouts  30.2 us
    dot_general x1, matrix products, local(): jnp.dot(learn_hidden, full_down, preferred_element_type=jnp.float32)  13.4 us
    dot_general x1, matrix products, local(): lax.dot_general(learn_hidden, rounded, (((0,), (0,)), ((), ())), preferre...  12 us
    dot_general x1, matrix products, local(): jnp.dot(fresh_hidden, full_down, preferred_element_type=jnp.float32)  12 us
  transfers between devices with their start and end apart: 18, of which 17 were waited for; matrix products, arithmetic and copies ran while one was open for 7% of the time, Pallas kernels for 0%

profile of v1, /device:TPU:8, one launch (start us, length us, event | category | flops | bytes accessed | tf_op | source)
XLA Modules:
  0.0 589.4 jit_solution(14806851062818794630)
XLA Ops:
  7.3 9.7 %collective-permute-done = bf16[256,1024]{1,0:T(8,128)(2,1)S(1)} collective-permute-done((bf16[256,1024]{1,0:T(8,128)(2,1)}, bf16[256,1024]{1,0:T(8,128)(2,1)S(1)}, u32[]{:S(2)}, u32[]{:S(2)}) %collective-permute-start) | collective-permute-done | bytes 524320 | tf_op jit(solution)/shard_map/ppermute | solution.py:99
  17.0 9.5 %collective-permute-done.1 = bf16[256,1024]{1,0:T(8,128)(2,1)S(1)} collective-permute-done((bf16[256,1024]{1,0:T(8,128)(2,1)S(1)}, bf16[256,1024]{1,0:T(8,128)(2,1)S(1)}, u32[]{:S(2)}, u32[]{:S(2)}) %collective-permute-start.1) | collective-permute-done | bytes 524320 | tf_op jit(solution)/shard_map/ppermute | solution.py:99
  26.5 9.5 %collective-permute-done.2 = bf16[256,1024]{1,0:T(8,128)(2,1)S(1)} collective-permute-done((bf16[256,1024]{1,0:T(8,128)(2,1)S(1)}, bf16[256,1024]{1,0:T(8,128)(2,1)S(1)}, u32[]{:S(2)}, u32[]{:S(2)}) %collective-permute-start.2) | collective-permute-done | bytes 524320 | tf_op jit(solution)/shard_map/ppermute | solution.py:99
  36.0 9.5 %collective-permute-done.3 = bf16[256,1024]{1,0:T(8,128)(2,1)S(1)} collective-permute-done((bf16[256,1024]{1,0:T(8,128)(2,1)S(1)}, bf16[256,1024]{1,0:T(8,128)(2,1)S(1)}, u32[]{:S(2)}, u32[]{:S(2)}) %collective-permute-start.3) | collective-permute-done | bytes 524320 | tf_op jit(solution)/shard_map/ppermute | solution.py:99
  45.5 9.5 %collective-permute-done.4 = bf16[256,1024]{1,0:T(8,128)(2,1)S(1)} collective-permute-done((bf16[256,1024]{1,0:T(8,128)(2,1)S(1)}, bf16[256,1024]{1,0:T(8,128)(2,1)S(1)}, u32[]{:S(2)}, u32[]{:S(2)}) %collective-permute-start.4) | collective-permute-done | bytes 524320 | tf_op jit(solution)/shard_map/ppermute | solution.py:99
  55.0 9.5 %collective-permute-done.5 = bf16[256,1024]{1,0:T(8,128)(2,1)S(1)} collective-permute-done((bf16[256,1024]{1,0:T(8,128)(2,1)S(1)}, bf16[256,1024]{1,0:T(8,128)(2,1)S(1)}, u32[]{:S(2)}, u32[]{:S(2)}) %collective-permute-start.5) | collective-permute-done | bytes 524320 | tf_op jit(solution)/shard_map/ppermute | solution.py:99
  65.3 9.5 %collective-permute-done.6 = bf16[256,1024]{1,0:T(8,128)(2,1)S(1)} collective-permute-done((bf16[256,1024]{1,0:T(8,128)(2,1)S(1)}, bf16[256,1024]{1,0:T(8,128)(2,1)S(1)}, u32[]{:S(2)}, u32[]{:S(2)}) %collective-permute-start.6) | collective-permute-done | bytes 524320 | tf_op jit(solution)/shard_map/ppermute | solution.py:99
  75.7 9.5 %collective-permute-done.7 = bf16[256,1024]{1,0:T(8,128)(2,1)S(1)} collective-permute-done((bf16[256,1024]{1,0:T(8,128)(2,1)S(1)}, bf16[256,1024]{1,0:T(8,128)(2,1)S(1)}, u32[]{:S(2)}, u32[]{:S(2)}) %collective-permute-start.7) | collective-permute-done | bytes 524320 | tf_op jit(solution)/shard_map/ppermute | solution.py:99
  86.0 9.5 %collective-permute-done.8 = bf16[256,1024]{1,0:T(8,128)(2,1)S(1)} collective-permute-done((bf16[256,1024]{1,0:T(8,128)(2,1)S(1)}, bf16[256,1024]{1,0:T(8,128)(2,1)S(1)}, u32[]{:S(2)}, u32[]{:S(2)}) %collective-permute-start.8) | collective-permute-done | bytes 524320 | tf_op jit(solution)/shard_map/ppermute | solution.py:99
  96.3 9.5 %collective-permute-done.9 = bf16[256,1024]{1,0:T(8,128)(2,1)S(1)} collective-permute-done((bf16[256,1024]{1,0:T(8,128)(2,1)S(1)}, bf16[256,1024]{1,0:T(8,128)(2,1)S(1)}, u32[]{:S(2)}, u32[]{:S(2)}) %collective-permute-start.9) | collective-permute-done | bytes 524320 | tf_op jit(solution)/shard_map/ppermute | solution.py:99
  106.6 9.5 %collective-permute-done.10 = bf16[256,1024]{1,0:T(8,128)(2,1)S(1)} collective-permute-done((bf16[256,1024]{1,0:T(8,128)(2,1)S(1)}, bf16[256,1024]{1,0:T(8,128)(2,1)S(1)}, u32[]{:S(2)}, u32[]{:S(2)}) %collective-permute-start.10) | collective-permute-done | bytes 524320 | tf_op jit(solution)/shard_map/ppermute | solution.py:99
  116.9 9.5 %collective-permute-done.11 = bf16[256,1024]{1,0:T(8,128)(2,1)S(1)} collective-permute-done((bf16[256,1024]{1,0:T(8,128)(2,1)S(1)}, bf16[256,1024]{1,0:T(8,128)(2,1)S(1)}, u32[]{:S(2)}, u32[]{:S(2)}) %collective-permute-start.11) | collective-permute-done | bytes 524320 | tf_op jit(solution)/shard_map/ppermute | solution.py:99
  127.2 9.5 %collective-permute-done.12 = bf16[256,1024]{1,0:T(8,128)(2,1)S(1)} collective-permute-done((bf16[256,1024]{1,0:T(8,128)(2,1)S(1)}, bf16[256,1024]{1,0:T(8,128)(2,1)S(1)}, u32[]{:S(2)}, u32[]{:S(2)}) %collective-permute-start.12) | collective-permute-done | bytes 524320 | tf_op jit(solution)/shard_map/ppermute | solution.py:99
  137.5 9.6 %collective-permute-done.13 = bf16[256,1024]{1,0:T(8,128)(2,1)} collective-permute-done((bf16[256,1024]{1,0:T(8,128)(2,1)S(1)}, bf16[256,1024]{1,0:T(8,128)(2,1)}, u32[]{:S(2)}, u32[]{:S(2)}) %collective-permute-start.13) | collective-permute-done | bytes 524320 | tf_op jit(solution)/shard_map/ppermute | solution.py:99
  147.1 2.4 copy.20
  152.7 4.2 collective-permute-done.14
  159.1 1.1 constant_dynamic-update-slice_fusion.29
  170.9 13.4 %multiply_reduce_fusion.2 = (f32[640]{0:T(1024)S(1)}, f32[640,1024]{0,1:T(8,128)S(1)}) fusion(bf16[640,4096]{1,0:T(8,128)(2,1)} %param.14, bf16[8192,1024]{1,0:T(8,128)(2,1)S(1)} %constant_dynamic-update-slice_fusion, s32[]{:T(128)S(6)} %select_n.34, bf16[640,1024]{0,1:T(8,128)(2,1)S(1)} %copy-done.19), kind=kOutput, calls=%fused_computation.14 | convolution fusion | flops 5371330048 | bytes 17566212 | tf_op jit(solution)/shard_map/dot_general | solution.py:103
  184.4 1.2 fusion.15
  191.4 1.9 multiply_reduce_fusion
  193.9 1.1 copy-done.20
  195.1 12.0 %convolution_bitcast_fusion = f32[4096,1024]{0,1:T(8,128)} fusion(bf16[640,1024]{0,1:T(8,128)(2,1)S(1)} %fusion.9, bf16[640,4096]{1,0:T(8,128)(2,1)} %param.14), kind=kOutput, calls=%fused_computation | convolution fusion | flops 5368709120 | bytes 23330816 | tf_op jit(solution)/shard_map/dot_general | solution.py:131
  207.2 2.5 copy.19
  209.7 12.0 %multiply_reduce_fusion.3 = (f32[640]{0:T(1024)S(1)}, f32[1024,640]{1,0:T(8,128)}) fusion(bf16[640,1024]{0,1:T(8,128)(2,1)} %copy.19, bf16[640,4096]{1,0:T(8,128)(2,1)} %param.16, bf16[8192,1024]{1,0:T(8,128)(2,1)} %copy-done.22, s32[]{:T(128)S(6)} %select_n.34), kind=kOutput, calls=%fused_computation.18 | convolution fusion | flops 5371330048 | bytes 17566212 | tf_op jit(solution)/shard_map/dot_general | solution.py:106
  221.6 3.2 fusion.13
  224.8 182.7 %reduce-scatter.2.cloned.1.call-done = f32[256,1024]{0,1:T(8,128)} async-done(((f32[4096,1024]{0,1:T(8,128)}), f32[256,1024]{0,1:T(8,128)}) %reduce-scatter.2.cloned.1.call-update) | async-done | bytes 1048592 | tf_op jit(solution)/shard_map/reduce_scatter | solution.py:130
  407.6 10.3 %fusion.6 = bf16[640,4096]{1,0:T(8,128)(2,1)} fusion(bf16[640,1024]{0,1:T(8,128)(2,1)} %copy-done.20, bf16[8192,1024]{1,0:T(8,128)(2,1)} %copy-done.22, s32[]{:T(128)S(6)} %select_n.34), kind=kOutput, calls=%fused_computation.7 | convolution fusion | flops 5371330560 | bytes 14942212 | tf_op jit(solution)/shard_map/dot_general | solution.py:139
  417.9 3.7 fusion.10
  421.6 40.1 %psum.23 = f32[1024]{0:T(1024)} all-reduce(f32[1024]{0:T(1024)S(1)} %get-tuple-element.12), channel_id=1, replica_groups=mesh['dp'=16,'rep'=2] {'dp','rep'}, use_global_device_ids=true, to_apply=%region_12.13 | all-reduce | flops 1024 | bytes 8192 | tf_op jit(solution)/shard_map/psum | solution.py:129
  461.7 2.5 copy.23
  464.3 117.1 %all-reduce.21.cloned.1.call-done = f32[1024,19]{0,1:T(8,128)} async-done(((f32[1024,19]{0,1:T(8,128)}), f32[1024,19]{0,1:T(8,128)}) %all-reduce.21.cloned.1.call-update) | async-done | bytes 77840 | tf_op jit(solution)/shard_map/psum | solution.py:129
  581.4 1.5 copy.58
  (204 shorter events, 28.7 us)
Async XLA Ops:
  7.2 177.2 %copy-start = (bf16[1024,19]{0,1:T(8,128)(2,1)S(1)}, bf16[1024,19]{0,1:T(8,128)(2,1)}, u32[]{:S(2)}) copy-start(bf16[1024,19]{0,1:T(8,128)(2,1)} %param.18) | copy-start | bytes 116740
  7.2 160.8 %copy-start.2 = (bf16[256,1024]{1,0:T(8,128)(2,1)S(1)}, bf16[256,1024]{1,0:T(8,128)(2,1)}, u32[]{:S(2)}) copy-start(bf16[256,1024]{1,0:T(8,128)(2,1)} %param.17) | copy-start | bytes 1572868
  7.2 400.3 %reduce-scatter.2.cloned.1.call-start = ((), (), s32[]{:S(2)}) async-start(), calls=%async_computation.1 | async-start | bytes 17825792 | tf_op jit(solution)/shard_map/reduce_scatter | solution.py:130
  7.2 9.8 %collective-permute-start = (bf16[256,1024]{1,0:T(8,128)(2,1)}, bf16[256,1024]{1,0:T(8,128)(2,1)S(1)}, u32[]{:S(2)}, u32[]{:S(2)}) collective-permute-start(bf16[256,1024]{1,0:T(8,128)(2,1)} %param.17), channel_id=1, source_target_pairs={{0,2},{2,4},{4,6},{6,8},{8,10},{10,12},{12,14},{14,16},{16,18},{18... | collective-permute-start | bytes 1572872 | tf_op jit(solution)/shard_map/ppermute | solution.py:99
  17.0 9.5 %collective-permute-start.1 = (bf16[256,1024]{1,0:T(8,128)(2,1)S(1)}, bf16[256,1024]{1,0:T(8,128)(2,1)S(1)}, u32[]{:S(2)}, u32[]{:S(2)}) collective-permute-start(bf16[256,1024]{1,0:T(8,128)(2,1)S(1)} %collective-permute-done), channel_id=1, source_target_pairs={{0,2},{2,4},{4,6},{6,8},{8,10},{10,12},{12,14},{14,16},{16,18},{18... | collective-permute-start | bytes 1572872 | tf_op jit(solution)/shard_map/ppermute | solution.py:99
  26.5 9.5 %collective-permute-start.2 = (bf16[256,1024]{1,0:T(8,128)(2,1)S(1)}, bf16[256,1024]{1,0:T(8,128)(2,1)S(1)}, u32[]{:S(2)}, u32[]{:S(2)}) collective-permute-start(bf16[256,1024]{1,0:T(8,128)(2,1)S(1)} %collective-permute-done.1), channel_id=1, source_target_pairs={{0,2},{2,4},{4,6},{6,8},{8,10},{10,12},{12,14},{14,16},{16,18},{18... | collective-permute-start | bytes 1572872 | tf_op jit(solution)/shard_map/ppermute | solution.py:99
  36.0 9.5 %collective-permute-start.3 = (bf16[256,1024]{1,0:T(8,128)(2,1)S(1)}, bf16[256,1024]{1,0:T(8,128)(2,1)S(1)}, u32[]{:S(2)}, u32[]{:S(2)}) collective-permute-start(bf16[256,1024]{1,0:T(8,128)(2,1)S(1)} %collective-permute-done.2), channel_id=1, source_target_pairs={{0,2},{2,4},{4,6},{6,8},{8,10},{10,12},{12,14},{14,16},{16,18},{18... | collective-permute-start | bytes 1572872 | tf_op jit(solution)/shard_map/ppermute | solution.py:99
  45.5 9.5 %collective-permute-start.4 = (bf16[256,1024]{1,0:T(8,128)(2,1)S(1)}, bf16[256,1024]{1,0:T(8,128)(2,1)S(1)}, u32[]{:S(2)}, u32[]{:S(2)}) collective-permute-start(bf16[256,1024]{1,0:T(8,128)(2,1)S(1)} %collective-permute-done.3), channel_id=1, source_target_pairs={{0,2},{2,4},{4,6},{6,8},{8,10},{10,12},{12,14},{14,16},{16,18},{18... | collective-permute-start | bytes 1572872 | tf_op jit(solution)/shard_map/ppermute | solution.py:99
  55.0 9.5 %collective-permute-start.5 = (bf16[256,1024]{1,0:T(8,128)(2,1)S(1)}, bf16[256,1024]{1,0:T(8,128)(2,1)S(1)}, u32[]{:S(2)}, u32[]{:S(2)}) collective-permute-start(bf16[256,1024]{1,0:T(8,128)(2,1)S(1)} %collective-permute-done.4), channel_id=1, source_target_pairs={{0,2},{2,4},{4,6},{6,8},{8,10},{10,12},{12,14},{14,16},{16,18},{18... | collective-permute-start | bytes 1572872 | tf_op jit(solution)/shard_map/ppermute | solution.py:99
  65.3 9.5 %collective-permute-start.6 = (bf16[256,1024]{1,0:T(8,128)(2,1)S(1)}, bf16[256,1024]{1,0:T(8,128)(2,1)S(1)}, u32[]{:S(2)}, u32[]{:S(2)}) collective-permute-start(bf16[256,1024]{1,0:T(8,128)(2,1)S(1)} %collective-permute-done.5), channel_id=1, source_target_pairs={{0,2},{2,4},{4,6},{6,8},{8,10},{10,12},{12,14},{14,16},{16,18},{18... | collective-permute-start | bytes 1572872 | tf_op jit(solution)/shard_map/ppermute | solution.py:99
  75.7 9.5 %collective-permute-start.7 = (bf16[256,1024]{1,0:T(8,128)(2,1)S(1)}, bf16[256,1024]{1,0:T(8,128)(2,1)S(1)}, u32[]{:S(2)}, u32[]{:S(2)}) collective-permute-start(bf16[256,1024]{1,0:T(8,128)(2,1)S(1)} %collective-permute-done.6), channel_id=1, source_target_pairs={{0,2},{2,4},{4,6},{6,8},{8,10},{10,12},{12,14},{14,16},{16,18},{18... | collective-permute-start | bytes 1572872 | tf_op jit(solution)/shard_map/ppermute | solution.py:99
  86.0 9.5 %collective-permute-start.8 = (bf16[256,1024]{1,0:T(8,128)(2,1)S(1)}, bf16[256,1024]{1,0:T(8,128)(2,1)S(1)}, u32[]{:S(2)}, u32[]{:S(2)}) collective-permute-start(bf16[256,1024]{1,0:T(8,128)(2,1)S(1)} %collective-permute-done.7), channel_id=1, source_target_pairs={{0,2},{2,4},{4,6},{6,8},{8,10},{10,12},{12,14},{14,16},{16,18},{18... | collective-permute-start | bytes 1572872 | tf_op jit(solution)/shard_map/ppermute | solution.py:99
  96.3 9.5 %collective-permute-start.9 = (bf16[256,1024]{1,0:T(8,128)(2,1)S(1)}, bf16[256,1024]{1,0:T(8,128)(2,1)S(1)}, u32[]{:S(2)}, u32[]{:S(2)}) collective-permute-start(bf16[256,1024]{1,0:T(8,128)(2,1)S(1)} %collective-permute-done.8), channel_id=1, source_target_pairs={{0,2},{2,4},{4,6},{6,8},{8,10},{10,12},{12,14},{14,16},{16,18},{18... | collective-permute-start | bytes 1572872 | tf_op jit(solution)/shard_map/ppermute | solution.py:99
  106.6 9.5 %collective-permute-start.10 = (bf16[256,1024]{1,0:T(8,128)(2,1)S(1)}, bf16[256,1024]{1,0:T(8,128)(2,1)S(1)}, u32[]{:S(2)}, u32[]{:S(2)}) collective-permute-start(bf16[256,1024]{1,0:T(8,128)(2,1)S(1)} %collective-permute-done.9), channel_id=1, source_target_pairs={{0,2},{2,4},{4,6},{6,8},{8,10},{10,12},{12,14},{14,16},{16,18},{18... | collective-permute-start | bytes 1572872 | tf_op jit(solution)/shard_map/ppermute | solution.py:99
  116.9 9.5 %collective-permute-start.11 = (bf16[256,1024]{1,0:T(8,128)(2,1)S(1)}, bf16[256,1024]{1,0:T(8,128)(2,1)S(1)}, u32[]{:S(2)}, u32[]{:S(2)}) collective-permute-start(bf16[256,1024]{1,0:T(8,128)(2,1)S(1)} %collective-permute-done.10), channel_id=1, source_target_pairs={{0,2},{2,4},{4,6},{6,8},{8,10},{10,12},{12,14},{14,16},{16,18},{18... | collective-permute-start | bytes 1572872 | tf_op jit(solution)/shard_map/ppermute | solution.py:99
  127.2 9.5 %collective-permute-start.12 = (bf16[256,1024]{1,0:T(8,128)(2,1)S(1)}, bf16[256,1024]{1,0:T(8,128)(2,1)S(1)}, u32[]{:S(2)}, u32[]{:S(2)}) collective-permute-start(bf16[256,1024]{1,0:T(8,128)(2,1)S(1)} %collective-permute-done.11), channel_id=1, source_target_pairs={{0,2},{2,4},{4,6},{6,8},{8,10},{10,12},{12,14},{14,16},{16,18},{18... | collective-permute-start | bytes 1572872 | tf_op jit(solution)/shard_map/ppermute | solution.py:99
  137.5 9.6 %collective-permute-start.13 = (bf16[256,1024]{1,0:T(8,128)(2,1)S(1)}, bf16[256,1024]{1,0:T(8,128)(2,1)}, u32[]{:S(2)}, u32[]{:S(2)}) collective-permute-start(bf16[256,1024]{1,0:T(8,128)(2,1)S(1)} %collective-permute-done.12), channel_id=1, source_target_pairs={{0,2},{2,4},{4,6},{6,8},{8,10},{10,12},{12,14},{14,16},{16,18},{18... | collective-permute-start | bytes 1572872 | tf_op jit(solution)/shard_map/ppermute | solution.py:99
  147.1 9.8 %collective-permute-start.14 = (bf16[256,1024]{1,0:T(8,128)(2,1)}, bf16[256,1024]{1,0:T(8,128)(2,1)}, u32[]{:S(2)}, u32[]{:S(2)}) collective-permute-start(bf16[256,1024]{1,0:T(8,128)(2,1)} %collective-permute-done.13), channel_id=1, source_target_pairs={{0,2},{2,4},{4,6},{6,8},{8,10},{10,12},{12,14},{14,16},{16,18},{18... | collective-permute-start | bytes 1572872 | tf_op jit(solution)/shard_map/ppermute | solution.py:99
  151.8 18.3 %copy-start.18 = (bf16[256,1024]{1,0:T(8,128)(2,1)S(1)}, bf16[256,1024]{1,0:T(8,128)(2,1)}, u32[]{:S(2)}) copy-start(bf16[256,1024]{1,0:T(8,128)(2,1)} %copy-done.17) | copy-start | bytes 1572868
  151.9 18.4 %copy-start.16 = (bf16[256,1024]{1,0:T(8,128)(2,1)S(1)}, bf16[256,1024]{1,0:T(8,128)(2,1)}, u32[]{:S(2)}) copy-start(bf16[256,1024]{1,0:T(8,128)(2,1)} %copy-done.15) | copy-start | bytes 1572868
  151.9 18.4 %copy-start.14 = (bf16[256,1024]{1,0:T(8,128)(2,1)S(1)}, bf16[256,1024]{1,0:T(8,128)(2,1)}, u32[]{:S(2)}) copy-start(bf16[256,1024]{1,0:T(8,128)(2,1)} %copy-done.13) | copy-start | bytes 1572868
  151.9 18.4 %copy-start.12 = (bf16[256,1024]{1,0:T(8,128)(2,1)S(1)}, bf16[256,1024]{1,0:T(8,128)(2,1)}, u32[]{:S(2)}) copy-start(bf16[256,1024]{1,0:T(8,128)(2,1)} %copy-done.11) | copy-start | bytes 1572868
  151.9 18.5 %copy-start.10 = (bf16[256,1024]{1,0:T(8,128)(2,1)S(1)}, bf16[256,1024]{1,0:T(8,128)(2,1)}, u32[]{:S(2)}) copy-start(bf16[256,1024]{1,0:T(8,128)(2,1)} %copy-done.9) | copy-start | bytes 1572868
  151.9 18.5 %copy-start.8 = (bf16[256,1024]{1,0:T(8,128)(2,1)S(1)}, bf16[256,1024]{1,0:T(8,128)(2,1)}, u32[]{:S(2)}) copy-start(bf16[256,1024]{1,0:T(8,128)(2,1)} %copy-done.7) | copy-start | bytes 1572868
  151.9 18.6 %copy-start.6 = (bf16[256,1024]{1,0:T(8,128)(2,1)S(1)}, bf16[256,1024]{1,0:T(8,128)(2,1)}, u32[]{:S(2)}) copy-start(bf16[256,1024]{1,0:T(8,128)(2,1)} %copy-done.5) | copy-start | bytes 1572868
  151.9 18.6 %copy-start.4 = (bf16[256,1024]{1,0:T(8,128)(2,1)S(1)}, bf16[256,1024]{1,0:T(8,128)(2,1)}, u32[]{:S(2)}) copy-start(bf16[256,1024]{1,0:T(8,128)(2,1)} %copy-done.3) | copy-start | bytes 1572868
  152.7 18.1 %copy-start.19 = (bf16[640,1024]{0,1:T(8,128)(2,1)S(1)}, bf16[640,1024]{0,1:T(8,128)(2,1)}, u32[]{:S(2)}) copy-start(bf16[640,1024]{0,1:T(8,128)(2,1)} %copy.20) | copy-start | bytes 3932164
  170.9 15.1 %copy-start.24 = (s32[8,80]{1,0:T(8,128)S(1)}, s32[8,80]{1,0:T(8,128)}, u32[]{:S(2)}) copy-start(s32[8,80]{1,0:T(8,128)} %param.23) | copy-start | bytes 7684
  170.9 15.1 %copy-start.25 = (f32[8,80]{1,0:T(8,128)S(1)}, f32[8,80]{1,0:T(8,128)}, u32[]{:S(2)}) copy-start(f32[8,80]{1,0:T(8,128)} %param.22) | copy-start | bytes 7684
  191.0 16.2 %copy-start.23 = (f32[8,80]{1,0:T(8,128)}, f32[8,80]{1,0:T(8,128)S(1)}, u32[]{:S(2)}) copy-start(f32[8,80]{1,0:T(8,128)S(1)} %get-tuple-element.42) | copy-start | bytes 7684
  207.1 254.6 %all-reduce.19.cloned.1.call-start = ((), (), s32[]{:S(2)}) async-start(), calls=%async_computation.2 | async-start | bytes 2097152 | tf_op jit(solution)/shard_map/psum | solution.py:138
  407.6 173.8 %all-reduce.21.cloned.1.call-start = ((), (), s32[]{:S(2)}) async-start(), calls=%async_computation.3 | async-start | bytes 196608 | tf_op jit(solution)/shard_map/psum | solution.py:129
  (14 other events, 76.3 us)
Sparse Core Ops, SparseCore 0:
  207.3 200.2 reduce-scatter.1
  409.8 40.8 all-reduce.18
  456.9 124.4 all-reduce.20
